TPU v7x, 512 devices: a whole 4x4x16 slice. The times are simulated.
512 devices in a mesh: dp: 8 (over x, core), seq: 64 (over y, z).
Axes of the slice: x: 4, y: 4, z: 16, core: 2. Of those that a mesh axis runs over, the one named last changes fastest.
Arguments:
- tokens: bfloat16 [131072, 512], P(('dp', 'seq')), parts along dimension 0, may hold values from -16 to 16
- globals_in: bfloat16 [1024, 512], P('dp'), parts along dimension 0, may hold values from -16 to 16
- seg_ids: int32 [131072], P(('dp', 'seq')), parts along dimension 0, may hold values from 1 to 63, as said below
- global_table: int32 [1024], P('dp'), parts along dimension 0, may hold values from 1 to 63
- w_qkv: bfloat16 [2, 512, 1536], replicated, may hold values from -1 to 1
- w_out: bfloat16 [2, 512, 512], replicated, may hold values from -0.25 to 0.25
- gain_local: float32 [2, 512], replicated, may hold values from 0.5 to 1.5
- gain_global: float32 [2, 512], replicated, may hold values from 0.5 to 1.5
- seg_bias: float32 [2, 8], replicated, may hold values from 2 to 5
Outputs:
- local_out: bfloat16 [131072, 512], P(('dp', 'seq')), parts along dimension 0
- global_out: bfloat16 [1024, 512], P('dp'), parts along dimension 0
There are 8 independent parts, one for each index of `dp`. A program takes and returns all parts, laid end to end along the dimension named above; an argument that names none is the same for every part. Nothing has to cross between parts.
Inputs may be any that keep to these rules, and one draw needn't show every extreme that they name: `seg_ids`: the entity ids come in runs of 128 consecutive tokens (the first and last runs of a context are shorter).
All inputs are finite; a program needn't handle non-finite values.
Results may differ from a plain program's by a relative error of at most 0.006.
Values may be sent and summed in bfloat16 or wider, within the bound.
No kernel may reach another device: no remote copies, remote signals or barrier semaphores. Data moves between devices by JAX's collectives and lax.ppermute only.
A program may use at most 192 MiB of HBM per device.

v0:
```python
import math

import jax
import jax.numpy as jnp
from jax import lax
from jax.sharding import PartitionSpec as P

RADIUS = 256
LAYERS = 2


masked_fill = -1e30


def with_halo(block, sides, width):
    for axis, dim in sides:
        count = lax.axis_size(axis)
        forward = [(i, i + 1) for i in range(count - 1)]
        backward = [(target, source) for source, target in forward]
        low = lax.ppermute(
            lax.slice_in_dim(block, block.shape[dim] - width, None, axis=dim), axis, forward
        )
        high = lax.ppermute(lax.slice_in_dim(block, 0, width, axis=dim), axis, backward)
        block = jnp.concatenate([low, block, high], axis=dim)
    return block


def layer_norm(values, gain):
    average = jnp.mean(values, axis=-1, keepdims=True)
    centered = values - average
    variance = jnp.mean(centered * centered, axis=-1, keepdims=True)
    return (centered * lax.rsqrt(variance + 1e-05) * gain).astype(jnp.bfloat16)


def window_attend(
    queries, keys_ext, values_ext, seg_rows, seg_ext, valid, gkeys, gvalues, bias, scaling
):
    rows = queries.shape[0]
    span = keys_ext.shape[0]
    radius = (span - rows) // 2
    scores = (
        jnp.einsum("thd,shd->hts", queries, keys_ext, preferred_element_type=jnp.float32) * scaling
    )
    offset = (
        jnp.arange(span, dtype=jnp.int32)[None, :]
        - radius
        - jnp.arange(rows, dtype=jnp.int32)[:, None]
    )
    allowed = (jnp.abs(offset) <= radius) & valid[None, :]
    same = (seg_rows[:, None] == seg_ext[None, :]).astype(jnp.float32)
    scores = scores + bias[:, None, None] * same[None]
    scores = jnp.where(allowed[None], scores, masked_fill)
    gscores = (
        jnp.einsum("thd,ghd->htg", queries, gkeys, preferred_element_type=jnp.float32) * scaling
    )
    top = jnp.maximum(jnp.max(scores, axis=-1), jnp.max(gscores, axis=-1))
    probs = jnp.exp(scores - top[..., None])
    gprobs = jnp.exp(gscores - top[..., None])
    total = jnp.sum(probs, axis=-1) + jnp.sum(gprobs, axis=-1)
    mixed = jnp.einsum(
        "hts,shd->thd", probs.astype(jnp.bfloat16), values_ext, preferred_element_type=jnp.float32
    )
    mixed = mixed + jnp.einsum(
        "htg,ghd->thd", gprobs.astype(jnp.bfloat16), gvalues, preferred_element_type=jnp.float32
    )
    return (mixed / jnp.transpose(total)[:, :, None]).reshape(rows, -1).astype(jnp.bfloat16)


def partial_global(gqueries, keys_loc, values_loc, seg_rows, table, scaling):
    scores = (
        jnp.einsum("ghd,thd->ght", gqueries, keys_loc, preferred_element_type=jnp.float32) * scaling
    )
    member = (table[:, None] == seg_rows[None, :])[:, None, :]
    scores = jnp.where(member, scores, masked_fill)
    top = jnp.max(scores, axis=-1)
    probs = jnp.where(member, jnp.exp(scores - top[..., None]), jnp.float32(0.0))
    total = jnp.sum(probs, axis=-1)
    weighted = jnp.einsum(
        "ght,thd->ghd", probs, values_loc.astype(jnp.float32), precision=lax.Precision.HIGHEST
    )
    return (top, total, weighted)


def self_global(gqueries, gkeys, gvalues, scaling):
    scores = (
        jnp.einsum("ghd,khd->ghk", gqueries, gkeys, preferred_element_type=jnp.float32) * scaling
    )
    top = jnp.max(scores, axis=-1)
    probs = jnp.exp(scores - top[..., None])
    total = jnp.sum(probs, axis=-1)
    weighted = jnp.einsum(
        "ghk,khd->ghd", probs, gvalues.astype(jnp.float32), precision=lax.Precision.HIGHEST
    )
    return (top, total, weighted)


def combine_parts(first, second):
    top = jnp.maximum(first[0], second[0])
    factor_a = jnp.exp(first[0] - top)
    factor_b = jnp.exp(second[0] - top)
    total = first[1] * factor_a + second[1] * factor_b
    weighted = first[2] * factor_a[..., None] + second[2] * factor_b[..., None]
    return (top, total, weighted)


def per_device(
    tokens, globals_in, seg_ids, global_table, w_qkv, w_out, gain_local, gain_global, seg_bias
):
    rows = tokens.shape[0]
    width = tokens.shape[1]
    heads = seg_bias.shape[1]
    head_dim = width // heads
    globals_count = globals_in.shape[0]
    scaling = 1.0 / math.sqrt(head_dim)
    shard = lax.axis_index("seq")
    shards = lax.axis_size("seq")
    seg_ext = with_halo(seg_ids, (("seq", 0),), RADIUS)
    position = shard * rows - RADIUS + jnp.arange(rows + 2 * RADIUS, dtype=jnp.int32)
    valid = (position >= 0) & (position < shards * rows)
    stream = tokens.astype(jnp.float32)
    gstate = globals_in.astype(jnp.float32)
    for layer_no in range(LAYERS):
        weight_in = w_qkv[layer_no]
        normed = layer_norm(stream, gain_local[layer_no])
        gnormed = layer_norm(gstate, gain_global[layer_no])
        proj = jnp.dot(normed, weight_in, preferred_element_type=jnp.float32).astype(jnp.bfloat16)
        gproj = jnp.dot(gnormed, weight_in, preferred_element_type=jnp.float32).astype(jnp.bfloat16)
        kv_ext = with_halo(proj[:, width:], (("seq", 0),), RADIUS)
        queries = proj[:, :width].reshape(rows, heads, head_dim)
        keys_ext = kv_ext[:, :width].reshape(-1, heads, head_dim)
        values_ext = kv_ext[:, width:].reshape(-1, heads, head_dim)
        gqueries = gproj[:, :width].reshape(globals_count, heads, head_dim)
        gkeys = gproj[:, width : 2 * width].reshape(globals_count, heads, head_dim)
        gvalues = gproj[:, 2 * width :].reshape(globals_count, heads, head_dim)
        local_mix = window_attend(
            queries,
            keys_ext,
            values_ext,
            seg_ids,
            seg_ext,
            valid,
            gkeys,
            gvalues,
            seg_bias[layer_no],
            scaling,
        )
        top, total, weighted = partial_global(
            gqueries,
            proj[:, width : 2 * width].reshape(rows, heads, head_dim),
            proj[:, 2 * width :].reshape(rows, heads, head_dim),
            seg_ids,
            global_table,
            scaling,
        )
        top_all = lax.pmax(top, "seq")
        factor = jnp.exp(top - top_all)
        total_all, weighted_all = lax.psum((total * factor, weighted * factor[..., None]), "seq")
        outer = (top_all, total_all, weighted_all)
        inner = self_global(gqueries, gkeys, gvalues, scaling)
        merged = combine_parts(outer, inner)
        global_mix = (
            (merged[2] / merged[1][..., None]).reshape(globals_count, width).astype(jnp.bfloat16)
        )
        stream = stream + jnp.dot(local_mix, w_out[layer_no], preferred_element_type=jnp.float32)
        gstate = gstate + jnp.dot(global_mix, w_out[layer_no], preferred_element_type=jnp.float32)
    return (stream.astype(jnp.bfloat16), gstate.astype(jnp.bfloat16))


def solution(mesh):
    return jax.shard_map(
        per_device,
        mesh=mesh,
        in_specs=(
            P(("dp", "seq"), None),
            P("dp", None),
            P(("dp", "seq")),
            P("dp"),
            P(),
            P(),
            P(),
            P(),
            P(),
        ),
        out_specs=(P(("dp", "seq"), None), P("dp", None)),
        check_vma=False,
    )
```

profile of v0, /device:TPU:2, one launch (start us, length us, event | category | flops | bytes accessed | tf_op | source)
XLA Modules:
  0.0 910.2 jit_solution(4620420478390181222)
XLA Ops:
  8.0 1.1 convert_reduce_fusion
  9.1 1.2 fusion.69
  10.3 2.1 convolution_convert_fusion.1
  13.3 4.6 collective-permute-start
  17.9 1.3 collective-permute-start.1
  19.2 4.5 collective-permute-start.2
  23.8 1.3 collective-permute-start.3
  25.6 1.8 convolution_convert_fusion.3
  28.9 150.6 %pmax.14 = f32[128,8]{0,1:T(8,128)S(1)} all-reduce(f32[128,8]{0,1:T(8,128)S(1)} %get-tuple-element.40), channel_id=1, replica_groups=mesh['dp'=8,'seq'=64] {'seq'}, use_global_device_ids=true, to_apply=%region_12.13 | all-reduce | flops 1024 | bytes 8192 | tf_op jit(solution)/shard_map/pmax | solution.py:155
  180.0 1.6 fusion.41
  181.8 138.2 %psum.29 = f32[128,8]{0,1:T(8,128)S(1)} all-reduce(f32[128,8]{0,1:T(8,128)S(1)} %get-tuple-element.10), channel_id=1, replica_groups=mesh['dp'=8,'seq'=64] {'seq'}, use_global_device_ids=true, to_apply=%region_16.17 | all-reduce | flops 1024 | bytes 8192 | tf_op jit(solution)/shard_map/psum | solution.py:157
  321.9 1.7 copy.45
  323.7 113.2 %all-reduce.3.cloned.1.call-done = f32[128,8,64]{0,2,1:T(8,128)} async-done(((f32[128,8,64]{0,2,1:T(8,128)}), f32[128,8,64]{0,2,1:T(8,128)}) %all-reduce.3.cloned.1.call-update) | async-done | bytes 262160 | tf_op jit(solution)/shard_map/psum | solution.py:157
  436.9 1.4 fusion.46
  438.4 1.2 fusion.145
  440.3 1.9 convolution_convert_fusion.2
  443.1 1.1 copy.60
  444.1 1.7 copy.56
  446.9 1.5 pad_maximum_fusion
  448.4 1.3 fusion.135
  449.7 2.3 copy.43
  452.0 3.3 fusion.4
  455.5 1.5 fusion.74
  457.1 1.1 copy-done.1
  458.2 2.1 fusion
  460.3 1.4 copy.41
  461.7 5.1 fusion.57
  469.8 3.4 collective-permute-start.4
  473.2 1.3 collective-permute-start.5
  475.3 1.4 fusion.149
  476.7 141.6 %pmax.15 = f32[128,8]{0,1:T(8,128)S(1)} all-reduce(f32[128,8]{0,1:T(8,128)S(1)} %get-tuple-element.52), channel_id=1, replica_groups=mesh['dp'=8,'seq'=64] {'seq'}, use_global_device_ids=true, to_apply=%region_24.25 | all-reduce | flops 1024 | bytes 8192 | tf_op jit(solution)/shard_map/pmax | solution.py:155
  618.8 1.8 copy.58
  620.5 2.6 fusion.42
  623.2 1.8 copy.48
  625.0 1.3 fusion.147
  626.3 138.0 %psum.31 = f32[128,8]{0,1:T(8,128)S(1)} all-reduce(f32[128,8]{0,1:T(8,128)S(1)} %get-tuple-element.5), channel_id=1, replica_groups=mesh['dp'=8,'seq'=64] {'seq'}, use_global_device_ids=true, to_apply=%region_28.29 | all-reduce | flops 1024 | bytes 8192 | tf_op jit(solution)/shard_map/psum | solution.py:157
  764.3 114.0 %all-reduce.5.cloned.1.call-done = f32[128,8,64]{0,2,1:T(8,128)} async-done(((f32[128,8,64]{0,2,1:T(8,128)}), f32[128,8,64]{0,2,1:T(8,128)}) %all-reduce.5.cloned.1.call-update) | async-done | bytes 262160 | tf_op jit(solution)/shard_map/psum | solution.py:157
  878.3 1.6 fusion.47
  879.9 1.9 fusion.45
  881.8 1.5 pad_maximum_fusion.1
  883.3 1.3 fusion.134
  884.5 2.3 copy.49
  886.9 3.4 fusion.5
  890.5 1.5 fusion.72
  892.0 1.1 copy-done
  893.1 2.8 fusion.2
  895.9 1.4 copy.47
  897.3 5.0 fusion.51
  (105 shorter events, 14.4 us)
Async XLA Ops:
  7.2 21.1 %copy-start.14 = (s32[256]{0:T(256)S(1)}, s32[256]{0:T(256)}, u32[]{:S(2)}) copy-start(s32[256]{0:T(256)} %param.11) | copy-start | bytes 3076
  7.2 18.1 %copy-start.15 = (f32[2,512]{1,0:T(2,128)S(1)}, f32[2,512]{1,0:T(2,128)}, u32[]{:S(2)}) copy-start(f32[2,512]{1,0:T(2,128)} %param.16) | copy-start | bytes 12292
  7.2 18.1 %copy-start.9 = (bf16[128,512]{1,0:T(8,128)(2,1)S(1)}, bf16[128,512]{1,0:T(8,128)(2,1)}, u32[]{:S(2)}) copy-start(bf16[128,512]{1,0:T(8,128)(2,1)} %param.10) | copy-start | bytes 393220
  7.2 21.1 %copy-start.19 = (s32[128]{0:T(128)S(1)}, s32[128]{0:T(128)}, u32[]{:S(2)}) copy-start(s32[128]{0:T(128)} %param.12) | copy-start | bytes 1540
  7.2 429.7 %all-reduce.3.cloned.1.call-start = ((), (), s32[]{:S(2)}) async-start(), calls=%async_computation | async-start | bytes 524288 | tf_op jit(solution)/shard_map/psum | solution.py:157
  13.3 433.0 %collective-permute-start = (bf16[256,1024]{1,0:T(8,128)(2,1)}, bf16[256,1024]{1,0:T(8,128)(2,1)}, u32[]{:S(2)}, u32[]{:S(2)}) collective-permute-start(bf16[256,1024]{1,0:T(8,128)(2,1)} %slice.114), channel_id=1, source_target_pairs={{0,1},{1,2},{2,3},{3,4},{4,5},{5,6},{6,7},{7,8},{8,9},{9,10},{10,1... | collective-permute-start | bytes 1572872 | tf_op jit(solution)/shard_map/ppermute | solution.py:20
  17.9 429.0 %collective-permute-start.1 = (bf16[256,1024]{1,0:T(8,128)(2,1)}, bf16[256,1024]{1,0:T(8,128)(2,1)}, u32[]{:S(2)}, u32[]{:S(2)}) collective-permute-start(bf16[256,1024]{1,0:T(8,128)(2,1)} %slice.114), channel_id=1, source_target_pairs={{1,0},{2,1},{3,2},{4,3},{5,4},{6,5},{7,6},{8,7},{9,8},{10,9},{11,1... | collective-permute-start | bytes 1572872 | tf_op jit(solution)/shard_map/ppermute | solution.py:23
  19.2 304.4 %collective-permute-start.2 = (s32[256]{0:T(256)}, s32[256]{0:T(256)S(1)}, u32[]{:S(2)}, u32[]{:S(2)}) collective-permute-start(s32[256]{0:T(256)} %param.11), channel_id=1, source_target_pairs={{0,1},{1,2},{2,3},{3,4},{4,5},{5,6},{6,7},{7,8},{8,9},{9,10},{10,1... | collective-permute-start | bytes 3080 | tf_op jit(solution)/shard_map/ppermute | solution.py:20
  23.8 299.8 %collective-permute-start.3 = (s32[256]{0:T(256)}, s32[256]{0:T(256)S(1)}, u32[]{:S(2)}, u32[]{:S(2)}) collective-permute-start(s32[256]{0:T(256)} %param.11), channel_id=1, source_target_pairs={{1,0},{2,1},{3,2},{4,3},{5,4},{6,5},{7,6},{8,7},{9,8},{10,9},{11,1... | collective-permute-start | bytes 3080 | tf_op jit(solution)/shard_map/ppermute | solution.py:23
  25.4 296.5 %copy-start.18 = (f32[2,8]{1,0:T(2,128)S(1)}, f32[2,8]{1,0:T(2,128)}, u32[]{:S(2)}) copy-start(f32[2,8]{1,0:T(2,128)} %param.17) | copy-start | bytes 196
  27.5 410.9 %copy-start.2 = (bf16[2,512,512]{2,1,0:T(8,128)(2,1)S(1)}, bf16[2,512,512]{2,1,0:T(8,128)(2,1)}, u32[]{:S(2)}) copy-start(bf16[2,512,512]{2,1,0:T(8,128)(2,1)} %param.14) | copy-start | bytes 3145732
  181.7 696.6 %all-reduce.5.cloned.1.call-start = ((), (), s32[]{:S(2)}) async-start(), calls=%async_computation.1 | async-start | bytes 524288 | tf_op jit(solution)/shard_map/psum | solution.py:157
  320.5 3.1 copy-start.11
  321.9 565.0 %copy-start.16 = (f32[8]{0:T(128)}, f32[8]{0:T(128)S(1)}, u32[]{:S(2)}) copy-start(f32[8]{0:T(128)S(1)} %get-tuple-element.32) | copy-start | bytes 100
  439.6 0.7 copy-start.4
  440.3 11.7 %copy-start.6 = (pred[256,768]{1,0:T(8,128)(4,1)S(1)}, pred[256,768]{1,0:T(8,128)(4,1)}, u32[]{:S(2)}) copy-start(pred[256,768]{1,0:T(8,128)(4,1)} %fusion.66) | copy-start | bytes 589828
  443.0 12.3 %copy-start.10 = (bf16[128,512]{0,1:T(8,128)(2,1)}, bf16[128,512]{0,1:T(8,128)(2,1)S(1)}, u32[]{:S(2)}) copy-start(bf16[128,512]{0,1:T(8,128)(2,1)S(1)} %copy.55) | copy-start | bytes 393220
  444.1 11.2 %copy-start.8 = (bf16[128,512]{0,1:T(8,128)(2,1)}, bf16[128,512]{0,1:T(8,128)(2,1)S(1)}, u32[]{:S(2)}) copy-start(bf16[128,512]{0,1:T(8,128)(2,1)S(1)} %copy.60) | copy-start | bytes 393220
  446.2 0.8 copy-start.5
  452.0 3.5 copy-start.13
  455.4 2.8 copy-start.1
  461.7 5.1 copy-start.3
  461.7 5.7 copy-start.20
  469.8 412.0 %collective-permute-start.4 = (bf16[256,1024]{1,0:T(8,128)(2,1)}, bf16[256,1024]{1,0:T(8,128)(2,1)}, u32[]{:S(2)}, u32[]{:S(2)}) collective-permute-start(bf16[256,1024]{1,0:T(8,128)(2,1)} %slice.120), channel_id=1, source_target_pairs={{0,1},{1,2},{2,3},{3,4},{4,5},{5,6},{6,7},{7,8},{8,9},{9,10},{10,1... | collective-permute-start | bytes 1572872 | tf_op jit(solution)/shard_map/ppermute | solution.py:20
  473.2 408.6 %collective-permute-start.5 = (bf16[256,1024]{1,0:T(8,128)(2,1)}, bf16[256,1024]{1,0:T(8,128)(2,1)}, u32[]{:S(2)}, u32[]{:S(2)}) collective-permute-start(bf16[256,1024]{1,0:T(8,128)(2,1)} %slice.120), channel_id=1, source_target_pairs={{1,0},{2,1},{3,2},{4,3},{5,4},{6,5},{7,6},{8,7},{9,8},{10,9},{11,1... | collective-permute-start | bytes 1572872 | tf_op jit(solution)/shard_map/ppermute | solution.py:23
  884.5 5.9 copy-start.12
  886.9 6.2 copy-start.7
  890.3 2.8 copy-start
  892.0 5.3 copy-start.17
Sparse Core Ops, SparseCore 0:
  181.8 255.0 all-reduce.2
  623.3 255.0 all-reduce.4
where the time goes:
time: 911 us; the launch traced here: 910 us
  blocking collectives  568 us (62%)
  waiting for transfers between devices  227 us (25%)
  matrix products  42.2 us (5%)
  local copies, waits for them, and re-layouts  27.9 us (3%)
  starting transfers between devices  16.5 us (2%)
  between operations  14.7 us (2%)
  other arithmetic  13.3 us (1%)
    pmax x2, blocking collectives, per_device(): top_all = lax.pmax(top, 'seq')  292 us
    psum x2, blocking collectives, per_device(): lax.psum((total * factor, weighted * factor[..., None]), 'seq')  276 us
    psum x2, waiting for transfers between devices, per_device(): lax.psum((total * factor, weighted * factor[..., None]), 'seq')  227 us
  transfers between devices with their start and end apart: 8, of which 2 were waited for; matrix products, arithmetic and copies ran while one was open for 4% of the time, Pallas kernels for 0%

commit v1 on v0

v1 whole, which is shorter than its diff:
```python
import functools
import math

import jax
import jax.numpy as jnp
from jax import lax
from jax.experimental import pallas as pl
from jax.experimental.pallas import tpu as pltpu
from jax.sharding import PartitionSpec as P

RADIUS = 256
LAYERS = 2
LANES = 128
ENTITIES = 64
NEG = -1e30
BF16 = jnp.bfloat16
F32 = jnp.float32

VMEM = pl.BlockSpec(memory_space=pltpu.VMEM)
SMEM = pl.BlockSpec(memory_space=pltpu.SMEM)


def dot(a, b):
    return jnp.dot(a, b, preferred_element_type=F32)


def dot_nt(a, b):
    return lax.dot_general(a, b, (((1,), (1,)), ((), ())), preferred_element_type=F32)


def dot_tn(a, b):
    return lax.dot_general(a, b, (((0,), (0,)), ((), ())), preferred_element_type=F32)


def norm_rows(values, gain):
    average = jnp.mean(values, axis=-1, keepdims=True)
    centered = values - average
    variance = jnp.mean(centered * centered, axis=-1, keepdims=True)
    return (centered * lax.rsqrt(variance + 1e-05) * gain).astype(BF16)


def one_hot(ids):
    rows = lax.broadcasted_iota(jnp.int32, (ENTITIES, ids.shape[1]), 0)
    return jnp.where(rows == ids, 1.0, 0.0).astype(BF16)


def half_of(shape):
    return lax.broadcasted_iota(jnp.int32, shape, len(shape) - 1) // (LANES // 2)


def project(normed, w_ref, first, count, store):
    for tile in range(first, first + count, 2):
        part = dot(normed, w_ref[:, tile * LANES : (tile + 2) * LANES]).astype(BF16)
        store(tile, part[:, :LANES])
        store(tile + 1, part[:, LANES:])


def split_three(value):
    high = value.astype(BF16).astype(F32)
    rest = value - high
    middle = rest.astype(BF16).astype(F32)
    return high, middle, rest - middle


def partial_pair(gq, keys, vals, member):
    rows = gq.shape[0]
    half = half_of((rows, LANES))
    out = jnp.zeros((rows, LANES), F32)
    marks = jnp.zeros((rows, LANES), F32)
    lane = lax.broadcasted_iota(jnp.int32, (rows, LANES), 1)
    for head in range(2):
        query = jnp.where(half == head, gq, jnp.zeros_like(gq))
        scores = jnp.where(member, dot_nt(query, keys), NEG)
        top = jnp.max(scores, axis=-1, keepdims=True)
        probs = jnp.where(member, jnp.exp(scores - top), 0.0)
        total = jnp.sum(probs, axis=-1, keepdims=True)
        weighted = dot(probs.astype(BF16), vals)
        some = total > 0.0
        safe = jnp.where(some, total, 1.0)
        out = jnp.where(half == head, weighted / safe, out)
        lse = jnp.where(some, top + jnp.log(safe), NEG)
        for part, piece in enumerate(split_three(lse)):
            marks = jnp.where(lane == head + 2 * part, piece, marks)
    return out, marks


def store_payload(payload, pair, out, marks):
    both = jnp.concatenate(
        [out.reshape(-1, 8, LANES), marks.reshape(-1, 8, LANES)], axis=1
    )
    payload[pair] = both.astype(BF16)


def global_parts(gproj, kv_at, member, payload, pairs):
    def step(pair, carry):
        gq = gproj[pair] * jnp.asarray(0.125, BF16)
        out, marks = partial_pair(gq, kv_at(0, pair), kv_at(1, pair), member)
        store_payload(payload, pair, out, marks)
        return carry

    for pair in range(pairs):
        step(pair, 0)


def first_kernel(
    tokens, globals_in, seg, table, gain_l, gain_g, w_qkv, payload, gproj, kv
):
    pairs = payload.shape[0]
    gnormed = norm_rows(globals_in[...].astype(F32), gain_g[...])

    def put_g(tile, part):
        gproj[tile] = part

    project(gnormed, w_qkv, 0, 3 * pairs, put_g)
    normed = norm_rows(tokens[...].astype(F32), gain_l[...])

    def put_kv(tile, part):
        kv[tile - pairs] = part

    project(normed, w_qkv, pairs, 2 * pairs, put_kv)
    member = dot_tn(one_hot(table[...]), one_hot(seg[...])) > 0.5
    global_parts(gproj, lambda which, pair: kv[which * pairs + pair], member, payload, pairs)


def second_kernel(
    mix, gstate, seg, table, gain_g, w_out, w_qkv, kv, payload, gproj, gstate_next
):
    pairs = payload.shape[0]
    state = gstate[...].astype(F32)
    for pair in range(pairs):
        state = state + dot(mix[pair], w_out[pair * LANES : (pair + 1) * LANES, :])
    gstate_next[...] = state
    gnormed = norm_rows(state, gain_g[...])

    def put_g(tile, part):
        gproj[tile] = part

    project(gnormed, w_qkv, 0, 3 * pairs, put_g)
    member = dot_tn(one_hot(table[...]), one_hot(seg[...])) > 0.5
    global_parts(gproj, lambda which, pair: kv[which * pairs + pair], member, payload, pairs)


def combine_kernel(where, parts, gproj, out):
    peers = parts.shape[0]
    pairs = gproj.shape[0] // 3
    pair = where[0]
    row = pl.multiple_of(where[1] * 8, 8)
    gq = gproj[pair, pl.ds(row, 8), :] * jnp.asarray(0.125, BF16)
    gk = gproj[pairs + pair]
    gv = gproj[2 * pairs + pair]
    half = half_of((8, LANES))
    own = jnp.zeros((8, LANES), F32)
    own_lse = jnp.zeros((8, LANES), F32)
    for head in range(2):
        query = jnp.where(half == head, gq, jnp.zeros_like(gq))
        scores = dot_nt(query, gk)
        top = jnp.max(scores, axis=-1, keepdims=True)
        probs = jnp.exp(scores - top)
        total = jnp.sum(probs, axis=-1, keepdims=True)
        own = jnp.where(half == head, dot(probs.astype(BF16), gv) / total, own)
        own_lse = jnp.where(half == head, top + jnp.log(total), own_lse)
    lane = lax.broadcasted_iota(jnp.int32, (LANES, LANES), 0)
    spread = jnp.where((lane < 6) & (lane % 2 == half_of((LANES, LANES))), 1.0, 0.0)
    both = parts[...].astype(F32)
    marks = both[:, 8:, :].reshape(peers * 8, LANES).astype(BF16)
    lse = dot(marks, spread.astype(BF16)).reshape(peers, 8, LANES)
    top = jnp.maximum(jnp.max(lse, axis=0), own_lse)
    weight = jnp.exp(lse - top[None])
    own_weight = jnp.exp(own_lse - top)
    total = jnp.sum(weight, axis=0) + own_weight
    mixed = jnp.sum(weight * both[:, :8, :], axis=0) + own_weight * own
    result = (mixed / total).astype(BF16)
    out[...] = jnp.broadcast_to(result[None], out.shape)


def last_kernel(mix, gstate, w_out, out):
    state = gstate[...]
    for pair in range(mix.shape[0]):
        state = state + dot(mix[pair], w_out[pair * LANES : (pair + 1) * LANES, :])
    out[...] = state.astype(BF16)


def attend(bias, layer_no, gproj, seg_lo, seg, seg_hi, queries, keys, vals, same, neg, mixed):
    pairs = queries.shape[0]
    rows = queries.shape[1]
    tile = rows // 2
    span = same.shape[2]
    globals_count = gproj.shape[1]
    for pair in range(pairs):
        for which, ref in ((1, keys), (2, vals)):
            block = gproj[which * pairs + pair]
            ref[pair, :globals_count, :] = block
            ref[pair, globals_count + rows + 2 * RADIUS :, :] = block
    ext = jnp.concatenate([seg_lo[...], seg[...], seg_hi[...]], axis=1)
    hot = one_hot(ext)
    alike = dot_tn(one_hot(seg[...]), hot)
    valid = jnp.where(ext > 0, 0.0, NEG)
    i = lax.broadcasted_iota(jnp.int32, (rows, rows + 2 * RADIUS), 0)
    e = lax.broadcasted_iota(jnp.int32, (rows, rows + 2 * RADIUS), 1)
    barred = jnp.where((e >= i) & (e <= i + 2 * RADIUS), valid, NEG)
    zeros = jnp.zeros((tile, globals_count), F32)
    local = span - globals_count
    same[0, :, :globals_count] = zeros
    neg[0, :, :globals_count] = zeros
    same[0, :, globals_count:] = alike[:tile, :local]
    neg[0, :, globals_count:] = barred[:tile, :local]
    same[1, :, :local] = alike[tile:, tile:]
    neg[1, :, :local] = barred[tile:, tile:]
    same[1, :, local:] = zeros
    neg[1, :, local:] = zeros

    half = half_of((tile, LANES))

    def step(pair, carry):
        for block in range(2):
            start = block * (globals_count + tile)
            q = queries[pair, block * tile : (block + 1) * tile, :]
            k = keys[pair, start : start + span, :]
            v = vals[pair, start : start + span, :]
            out = jnp.zeros((tile, LANES), F32)
            for head in range(2):
                query = jnp.where(half == head, q, jnp.zeros_like(q))
                boost = bias[layer_no, 2 * pair + head]
                scores = dot_nt(query, k) + (same[block] * boost + neg[block])
                top = jnp.max(scores, axis=-1, keepdims=True)
                probs = jnp.exp(scores - top)
                total = jnp.sum(probs, axis=-1, keepdims=True)
                out = jnp.where(half == head, dot(probs.astype(BF16), v) / total, out)
            mixed[pair, block * tile : (block + 1) * tile, :] = out.astype(BF16)
        return carry

    lax.fori_loop(0, pairs, step, 0)


def fill_rows(normed_parts, w_ref, pairs, globals_count, keys, vals):
    at = globals_count
    for normed in normed_parts:
        count = normed.shape[0]

        def put(tile, part, at=at, count=count):
            ref = keys if tile < 2 * pairs else vals
            ref[tile % pairs, at : at + count, :] = part

        project(normed, w_ref, pairs, 2 * pairs, put)
        at += count


def local_first(
    bias, tokens, low, high, seg_lo, seg, seg_hi, gproj, w_qkv, w_out, gain, next_gain,
    next_w, stream_out, normed_out, kv_out, queries, keys, vals, same, neg, mixed,
):
    pairs = queries.shape[0]
    globals_count = gproj.shape[1]
    scale = jnp.asarray(0.125, BF16)
    parts = [norm_rows(ref[...].astype(F32), gain[...]) for ref in (low, tokens, high)]

    def put_q(tile, part):
        queries[tile] = part * scale

    project(parts[1], w_qkv, 0, pairs, put_q)
    fill_rows(parts, w_qkv, pairs, globals_count, keys, vals)
    attend(bias, 0, gproj, seg_lo, seg, seg_hi, queries, keys, vals, same, neg, mixed)
    stream = tokens[...].astype(F32)
    for pair in range(pairs):
        stream = stream + dot(mixed[pair], w_out[pair * LANES : (pair + 1) * LANES, :])
    stream_out[...] = stream
    normed = norm_rows(stream, next_gain[...])
    normed_out[...] = normed

    def put_kv(tile, part):
        kv_out[tile - pairs] = part

    project(normed, next_w, pairs, 2 * pairs, put_kv)


def local_second(
    bias, normed, low, high, seg_lo, seg, seg_hi, gproj, w_qkv, w_out, stream, kv,
    out, queries, keys, vals, same, neg, mixed,
):
    pairs = queries.shape[0]
    globals_count = gproj.shape[1]
    rows = normed.shape[0]
    scale = jnp.asarray(0.125, BF16)

    def put_q(tile, part):
        queries[tile] = part * scale

    project(normed[...], w_qkv, 0, pairs, put_q)
    at = globals_count
    fill_rows([low[...]], w_qkv, pairs, at, keys, vals)
    fill_rows([high[...]], w_qkv, pairs, at + low.shape[0] + rows, keys, vals)
    for pair in range(pairs):
        keys[pair, at + RADIUS : at + RADIUS + rows, :] = kv[pair]
        vals[pair, at + RADIUS : at + RADIUS + rows, :] = kv[pairs + pair]
    attend(bias, 1, gproj, seg_lo, seg, seg_hi, queries, keys, vals, same, neg, mixed)
    total = stream[...]
    for pair in range(pairs):
        total = total + dot(mixed[pair], w_out[pair * LANES : (pair + 1) * LANES, :])
    out[...] = total.astype(BF16)


def call(kernel, name, out_shape, in_specs, cost, scratch=()):
    return pl.pallas_call(
        kernel,
        name=name,
        out_shape=out_shape,
        in_specs=in_specs,
        out_specs=jax.tree.map(lambda _: VMEM, out_shape),
        scratch_shapes=list(scratch),
        cost_estimate=pl.CostEstimate(flops=cost, bytes_accessed=4 << 20, transcendentals=0),
        compiler_params=pltpu.CompilerParams(vmem_limit_bytes=48 << 20),
    )


def per_device(
    tokens, globals_in, seg_ids, global_table, w_qkv, w_out, gain_local, gain_global, seg_bias
):
    rows, width = tokens.shape
    globals_count = globals_in.shape[0]
    shard = lax.axis_index("seq")
    shards = lax.axis_size("seq")
    pairs = width // LANES
    groups = globals_count // 8
    forward = [(i, i + 1) for i in range(shards - 1)]
    backward = [(i + 1, i) for i in range(shards - 1)]

    def halo(block):
        return lax.ppermute(block, "seq", forward), lax.ppermute(block, "seq", backward)

    def exchange(block):
        return lax.all_to_all(block, "seq", 0, 0, tiled=True)

    S = jax.ShapeDtypeStruct
    seg = seg_ids.reshape(1, rows)
    table = global_table.reshape(1, globals_count)
    where = jnp.stack([shard // groups, shard % groups]).astype(jnp.int32)
    payload_shape = S((pairs, groups, 16, LANES), BF16)
    gproj_shape = S((3 * pairs, globals_count, LANES), BF16)
    kv_shape = S((2 * pairs, rows, LANES), BF16)
    scratch = (
        pltpu.VMEM((pairs, rows, LANES), BF16),
        pltpu.VMEM((pairs, rows + 2 * RADIUS + 2 * globals_count, LANES), BF16),
        pltpu.VMEM((pairs, rows + 2 * RADIUS + 2 * globals_count, LANES), BF16),
        pltpu.VMEM((2, rows // 2, rows // 2 + 2 * RADIUS + globals_count), F32),
        pltpu.VMEM((2, rows // 2, rows // 2 + 2 * RADIUS + globals_count), F32),
        pltpu.VMEM((pairs, rows, LANES), BF16),
    )

    def combine(payload, gproj):
        parts = exchange(payload.reshape(shards, 16, LANES))
        mix = call(
            combine_kernel, "combine", S((shards, 8, LANES), BF16), [SMEM, VMEM, VMEM], 1 << 28
        )(where, parts, gproj)
        return exchange(mix).reshape(pairs, globals_count, LANES)

    tok_lo, tok_hi = halo(tokens)
    seg_lo, seg_hi = halo(seg)
    payload, gproj, _ = call(
        first_kernel, "parts_first", (payload_shape, gproj_shape, kv_shape), [VMEM] * 7, 1 << 30
    )(tokens, globals_in, seg, table, gain_local[0:1], gain_global[0:1], w_qkv[0])
    mix = combine(payload, gproj)
    stream, normed, kv = call(
        local_first,
        "local_first",
        (S((rows, width), F32), S((rows, width), BF16), kv_shape),
        [SMEM] + [VMEM] * 12,
        6 << 30,
        scratch,
    )(
        seg_bias, tokens, tok_lo, tok_hi, seg_lo, seg, seg_hi, gproj, w_qkv[0], w_out[0],
        gain_local[0:1], gain_local[1:2], w_qkv[1],
    )
    low, high = halo(normed)
    payload, gproj, gstate = call(
        second_kernel,
        "parts_second",
        (payload_shape, gproj_shape, S((globals_count, width), F32)),
        [VMEM] * 8,
        1 << 30,
    )(mix, globals_in, seg, table, gain_global[1:2], w_out[0], w_qkv[1], kv)
    mix = combine(payload, gproj)
    local_out = call(
        local_second, "local_second", S((rows, width), BF16), [SMEM] + [VMEM] * 11, 6 << 30,
        scratch,
    )(
        seg_bias, normed, low, high, seg_lo, seg, seg_hi, gproj, w_qkv[1], w_out[1], stream, kv
    )
    global_out = call(
        last_kernel, "last", S((globals_count, width), BF16), [VMEM] * 3, 1 << 28
    )(mix, gstate, w_out[1])
    return local_out, global_out


def solution(mesh):
    return jax.shard_map(
        per_device,
        mesh=mesh,
        in_specs=(
            P(("dp", "seq"), None),
            P("dp", None),
            P(("dp", "seq")),
            P("dp"),
            P(),
            P(),
            P(),
            P(),
            P(),
        ),
        out_specs=(P(("dp", "seq"), None), P("dp", None)),
        check_vma=False,
    )
```

time: 911 us -> 141 us (0.15)
  blocking collectives: 568 us -> 0 us
  waiting for transfers between devices: 227 us -> 28.3 us
  starting transfers between devices: 16.5 us -> 64.5 us
  matrix products: 42.2 us -> 0 us
  Pallas kernels: 0 us -> 28.7 us
  between operations: 14.7 us -> 0.94 us
  other arithmetic: 13.3 us -> 0.08 us
  local copies, waits for them, and re-layouts: 27.9 us -> 17.3 us
    pmax x2 -> x0, blocking collectives: 292 us -> none  [per_device(): top_all = lax.pmax(top, 'seq')]
    psum x2 -> x0, blocking collectives: 276 us -> none  [per_device(): lax.psum((total * factor, weighted * factor[..., None]), 'seq')]
    psum x2 -> x0, waiting for transfers between devices: 227 us -> none  [per_device(): lax.psum((total * factor, weighted * factor[..., None]), 'seq')]
    all_to_all x0 -> x4, starting transfers between devices: none -> 48.5 us  [exchange(): return lax.all_to_all(block, 'seq', 0, 0, tiled=True)]
    dot_general x24 -> x0, matrix products: 42.2 us -> none  [the longest x2 10.1 us: window_attend(): jnp.einsum('hts,shd->thd', probs.astype(jnp.bfloat16), values_ext, prefer...]
    pallas_call x0 -> x7, Pallas kernels: none -> 28.7 us  [the longest x1 9.33 us: per_device(): call(local_first, 'local_first', (S((rows, width), F32), S((rows, width),...]
    all_to_all x0 -> x4, waiting for transfers between devices: none -> 28.3 us  [exchange(): return lax.all_to_all(block, 'seq', 0, 0, tiled=True)]
    slice x26 -> x1, local copies, waits for them, and re-layouts: 24.4 us -> 0.01 us  [per_device(): gain_global[1:2]]
  transfers between devices with their start and end apart: 8 -> 10, of which waited for: 2 -> 4; matrix products, arithmetic and copies ran while one was open for 4% -> 1% of each run, Pallas kernels for 0% -> 16%
where the time goes in v1:
time: 141 us; the launch traced here: 140 us
  starting transfers between devices  64.5 us (46%)
  Pallas kernels  28.7 us (20%)
  waiting for transfers between devices  28.3 us (20%)
  local copies, waits for them, and re-layouts  17.3 us (12%)
    all_to_all x4, starting transfers between devices, exchange(): return lax.all_to_all(block, 'seq', 0, 0, tiled=True)  48.5 us
    all_to_all x4, waiting for transfers between devices, exchange(): return lax.all_to_all(block, 'seq', 0, 0, tiled=True)  28.3 us
    unnamed x50, local copies, waits for them, and re-layouts  13.9 us
    ppermute x3, starting transfers between devices, halo(): lax.ppermute(block, 'seq', forward)  12.1 us
    pallas_call x1, Pallas kernels, per_device(): call(local_first, 'local_first', (S((rows, width), F32), S((rows, width),...  9.33 us
    pallas_call x1, Pallas kernels, per_device(): call(local_second, 'local_second', S((rows, width), BF16), [SMEM] + [VMEM...  8.64 us
    pallas_call x2, Pallas kernels, combine(): call(combine_kernel, 'combine', S((shards, 8, LANES), BF16), [SMEM, VMEM,...  3.88 us
    ppermute x3, starting transfers between devices, halo(): lax.ppermute(block, 'seq', backward)  3.86 us
  transfers between devices with their start and end apart: 10, of which 4 were waited for; matrix products, arithmetic and copies ran while one was open for 1% of the time, Pallas kernels for 16%

profile of v1, /device:TPU:2, one launch (start us, length us, event | category | flops | bytes accessed | tf_op | source)
XLA Modules:
  0.0 139.8 jit_solution(15127119459294497013)
XLA Ops:
  0.7 0.0 copy-start.8
  0.7 0.0 copy-start.5
  0.7 2.1 %slice_bitcast_fusion = (bf16[512,1536]{1,0:T(8,128)(2,1)S(1)}, bf16[512,1536]{1,0:T(8,128)(2,1)S(1)}) fusion(bf16[2,512,1536]{2,1,0:T(8,128)(2,1)} %param.13), kind=kLoop, calls=%fused_computation | loop fusion | bytes 6291456 | tf_op jit(solution)/shard_map/squeeze | solution.py:371
  2.9 3.0 %parts_first.1 = (bf16[4,16,16,128]{3,2,1,0:T(8,128)(2,1)}, bf16[12,128,128]{2,1,0:T(8,128)(2,1)S(1)}, bf16[8,256,128]{2,1,0:T(8,128)(2,1)}) custom-call(bf16[256,512]{1,0:T(8,128)(2,1)S(1)} %copy-done.2, bf16[128,512]{1,0:T(8,128)(2,1)S(1)} %copy-done.5, s32[1,256]{1,0:T(1,128)} %bitcast.seg, s32[1,128]{1,0:T(1,128)S(1)} %bitcast.18, ...), custom_call_target="tpu_custom_call" | custom-call | flops 1073741824 | bytes 4194304 | tf_op jit(solution)/shard_map/parts_first/pallas_call | solution.py:358
  5.9 0.7 copy-done.12
  6.6 18.7 %all-to-all-start = ((bf16[64,16,128]{2,1,0:T(8,128)(2,1)}), bf16[64,16,128]{2,1,0:T(8,128)(2,1)S(1)}, u32[]{:S(2)}, u32[]{:S(2)}) async-start(bf16[64,16,128]{2,1,0:T(8,128)(2,1)} %bitcast.7), calls=%async_computation | async-start | bytes 524288 | tf_op jit(solution)/shard_map/all_to_all | solution.py:331
  25.4 4.0 %collective-permute-start.2 = (s32[1,256]{1,0:T(1,128)}, s32[1,256]{1,0:T(1,128)}, u32[]{:S(2)}, u32[]{:S(2)}) collective-permute-start(s32[1,256]{1,0:T(1,128)} %bitcast.seg), channel_id=1, source_target_pairs={{0,1},{1,2},{2,3},{3,4},{4,5},{5,6},{6,7},{7,8},{8,9},{9,10},{10,1... | collective-permute-start | bytes 3080 | tf_op jit(solution)/shard_map/ppermute | solution.py:328
  29.4 1.3 collective-permute-start.3
  30.7 4.6 %collective-permute-start = (bf16[256,512]{1,0:T(8,128)(2,1)S(1)}, bf16[256,512]{1,0:T(8,128)(2,1)S(1)}, u32[]{:S(2)}, u32[]{:S(2)}) collective-permute-start(bf16[256,512]{1,0:T(8,128)(2,1)S(1)} %copy-done.2), channel_id=1, source_target_pairs={{0,1},{1,2},{2,3},{3,4},{4,5},{5,6},{6,7},{7,8},{8,9},{9,10},{10,1... | collective-permute-start | bytes 786440 | tf_op jit(solution)/shard_map/ppermute | solution.py:328
  35.2 1.3 collective-permute-start.1
  36.6 0.1 pad_add_fusion.where
  36.6 1.3 slice_bitcast_fusion.2
  37.9 9.1 %all-to-all-done.parts = bf16[64,16,128]{2,1,0:T(8,128)(2,1)S(1)} async-done(((bf16[64,16,128]{2,1,0:T(8,128)(2,1)}), bf16[64,16,128]{2,1,0:T(8,128)(2,1)S(1)}, u32[]{:S(2)}, u32[]{:S(2)}) %all-to-all-start) | async-done | bytes 262176 | tf_op jit(solution)/shard_map/all_to_all | solution.py:331
  47.0 1.0 copy-done.13
  48.0 1.9 %combine.2 = bf16[64,8,128]{2,1,0:T(8,128)(2,1)} custom-call(s32[2]{0:T(128)S(1)} %pad_add_fusion.where, bf16[64,16,128]{2,1,0:T(8,128)(2,1)S(1)} %all-to-all-done.parts, bf16[12,128,128]{2,1,0:T(8,128)(2,1)S(1)} %copy-done.13), custom_call_target="tpu_custom_call" | custom-call | flops 268435456 | bytes 4194304 | tf_op jit(solution)/shard_map/combine/pallas_call | solution.py:351
  50.0 9.0 %all-to-all-start.1 = ((bf16[64,8,128]{2,1,0:T(8,128)(2,1)}), bf16[64,8,128]{2,1,0:T(8,128)(2,1)S(1)}, u32[]{:S(2)}, u32[]{:S(2)}) async-start(bf16[64,8,128]{2,1,0:T(8,128)(2,1)} %combine.2), calls=%async_computation.1 | async-start | bytes 262144 | tf_op jit(solution)/shard_map/all_to_all | solution.py:331
  59.0 0.0 collective-permute-done.2.seg_lo
  59.0 0.0 collective-permute-done.3.seg_hi
  59.0 0.0 collective-permute-done.low
  59.0 0.0 collective-permute-done.1.high
  59.0 1.4 %copy-done.1 = bf16[512,1536]{1,0:T(8,128)(2,1)S(1)} copy-done((bf16[512,1536]{1,0:T(8,128)(2,1)S(1)}, bf16[512,1536]{1,0:T(8,128)(2,1)}, u32[]{:S(2)}) %copy-start.1) | copy-done | bytes 1572888
  60.4 1.0 copy-done.14
  61.4 9.3 %local_first.1 = (f32[256,512]{1,0:T(8,128)S(1)}, bf16[256,512]{1,0:T(8,128)(2,1)S(1)}, bf16[8,256,128]{2,1,0:T(8,128)(2,1)S(1)}) custom-call(f32[2,8]{1,0:T(2,128)S(1)} %copy-done.7, bf16[256,512]{1,0:T(8,128)(2,1)S(1)} %copy-done.2, bf16[256,512]{1,0:T(8,128)(2,1)S(1)} %collective-permute-done.low, bf16[256,512]{1,0:T(8,128)(2,1)} %collective-permute-done.1.high, ...), custom_call_target="tpu_custom_call" | custom-call | flops 6442450944 | bytes 4194304 | tf_op jit(solution)/shard_map/local_first/pallas_call | solution.py:362
  70.8 0.0 copy-start.3
  70.8 0.7 copy-done.3
  71.5 0.8 copy-done.18
  72.3 0.8 copy-done.21
  73.1 1.1 all-to-all-done.1
  74.2 0.9 copy-done.6
  75.1 0.7 copy-done.9
  75.8 1.0 copy-done.19
  76.8 2.9 %parts_second.1 = (bf16[4,16,16,128]{3,2,1,0:T(8,128)(2,1)}, bf16[12,128,128]{2,1,0:T(8,128)(2,1)S(1)}, f32[128,512]{1,0:T(8,128)S(1)}) custom-call(bf16[4,128,128]{2,1,0:T(8,128)(2,1)S(1)} %bitcast.17, bf16[128,512]{1,0:T(8,128)(2,1)S(1)} %copy-done.6, s32[1,256]{1,0:T(1,128)} %bitcast.seg, s32[1,128]{1,0:T(1,128)S(1)} %bitcast.19, ...), custom_call_target="tpu_custom_call" | custom-call | flops 1073741824 | bytes 4194304 | tf_op jit(solution)/shard_map/parts_second/pallas_call | solution.py:374
  79.7 0.7 copy-done.15
  80.5 14.0 %all-to-all-start.2 = ((bf16[64,16,128]{2,1,0:T(8,128)(2,1)}), bf16[64,16,128]{2,1,0:T(8,128)(2,1)S(1)}, u32[]{:S(2)}, u32[]{:S(2)}) async-start(bf16[64,16,128]{2,1,0:T(8,128)(2,1)} %bitcast.10), calls=%async_computation.2 | async-start | bytes 524288 | tf_op jit(solution)/shard_map/all_to_all | solution.py:331
  94.5 3.5 %collective-permute-start.4 = (bf16[256,512]{1,0:T(8,128)(2,1)S(1)}, bf16[256,512]{1,0:T(8,128)(2,1)S(1)}, u32[]{:S(2)}, u32[]{:S(2)}) collective-permute-start(bf16[256,512]{1,0:T(8,128)(2,1)S(1)} %copy-done.4), channel_id=1, source_target_pairs={{0,1},{1,2},{2,3},{3,4},{4,5},{5,6},{6,7},{7,8},{8,9},{9,10},{10,1... | collective-permute-start | bytes 786440 | tf_op jit(solution)/shard_map/ppermute | solution.py:328
  98.0 1.3 collective-permute-start.5
  99.3 14.9 %all-to-all-done.2.parts = bf16[64,16,128]{2,1,0:T(8,128)(2,1)S(1)} async-done(((bf16[64,16,128]{2,1,0:T(8,128)(2,1)}), bf16[64,16,128]{2,1,0:T(8,128)(2,1)S(1)}, u32[]{:S(2)}, u32[]{:S(2)}) %all-to-all-start.2) | async-done | bytes 262176 | tf_op jit(solution)/shard_map/all_to_all | solution.py:331
  114.3 1.0 copy-done.16
  115.3 1.9 %combine.3 = bf16[64,8,128]{2,1,0:T(8,128)(2,1)} custom-call(s32[2]{0:T(128)S(1)} %copy-done.11, bf16[64,16,128]{2,1,0:T(8,128)(2,1)S(1)} %all-to-all-done.2.parts, bf16[12,128,128]{2,1,0:T(8,128)(2,1)S(1)} %copy-done.16), custom_call_target="tpu_custom_call" | custom-call | flops 268435456 | bytes 4194304 | tf_op jit(solution)/shard_map/combine/pallas_call | solution.py:351
  117.2 6.8 %all-to-all-start.3 = ((bf16[64,8,128]{2,1,0:T(8,128)(2,1)}), bf16[64,8,128]{2,1,0:T(8,128)(2,1)S(1)}, u32[]{:S(2)}, u32[]{:S(2)}) async-start(bf16[64,8,128]{2,1,0:T(8,128)(2,1)} %combine.3), calls=%async_computation.3 | async-start | bytes 262144 | tf_op jit(solution)/shard_map/all_to_all | solution.py:331
  124.0 0.0 collective-permute-done.4.low
  124.0 0.0 collective-permute-done.5.high
  124.0 1.0 copy-done.17
  125.0 1.0 copy-done.20
  126.0 1.0 copy-done.22
  127.1 8.6 %local_second.1 = bf16[256,512]{1,0:T(8,128)(2,1)} custom-call(f32[2,8]{1,0:T(2,128)S(1)} %copy-done.7, bf16[256,512]{1,0:T(8,128)(2,1)S(1)} %copy-done.4, bf16[256,512]{1,0:T(8,128)(2,1)S(1)} %collective-permute-done.4.low, bf16[256,512]{1,0:T(8,128)(2,1)S(1)} %collective-permute-done.5.high, s32[1,256]{1,0:T(1,128)} %collective-permute-done.2.seg_lo, ...), custom_call_target="tpu_custom_call" | custom-call | flops 6442450944 | bytes 4194304 | tf_op jit(solution)/shard_map/local_second/pallas_call | solution.py:382
  135.7 3.2 %all-to-all-done.3 = bf16[64,8,128]{2,1,0:T(8,128)(2,1)S(1)} async-done(((bf16[64,8,128]{2,1,0:T(8,128)(2,1)}), bf16[64,8,128]{2,1,0:T(8,128)(2,1)S(1)}, u32[]{:S(2)}, u32[]{:S(2)}) %all-to-all-start.3) | async-done | bytes 131104 | tf_op jit(solution)/shard_map/all_to_all | solution.py:331
  138.9 0.9 last.1
  (33 shorter events, 0.1 us)
Async XLA Ops:
  0.6 2.2 %copy-start.24 = (f32[2,512]{1,0:T(2,128)S(1)}, f32[2,512]{1,0:T(2,128)}, u32[]{:S(2)}) copy-start(f32[2,512]{1,0:T(2,128)} %param.15) | copy-start | bytes 12292
  0.6 2.2 %copy-start.23 = (f32[2,512]{1,0:T(2,128)S(1)}, f32[2,512]{1,0:T(2,128)}, u32[]{:S(2)}) copy-start(f32[2,512]{1,0:T(2,128)} %param.16) | copy-start | bytes 12292
  0.7 2.2 %copy-start.8 = (s32[128]{0:T(128)S(1)}, s32[128]{0:T(128)}, u32[]{:S(2)}) copy-start(s32[128]{0:T(128)} %param.12) | copy-start | bytes 1540
  0.7 2.2 %copy-start.5 = (bf16[128,512]{1,0:T(8,128)(2,1)S(1)}, bf16[128,512]{1,0:T(8,128)(2,1)}, u32[]{:S(2)}) copy-start(bf16[128,512]{1,0:T(8,128)(2,1)} %gstate.1) | copy-start | bytes 393220
  0.7 2.2 %copy-start.2 = (bf16[256,512]{1,0:T(8,128)(2,1)S(1)}, bf16[256,512]{1,0:T(8,128)(2,1)}, u32[]{:S(2)}) copy-start(bf16[256,512]{1,0:T(8,128)(2,1)} %tokens.3) | copy-start | bytes 786436
  2.8 3.0 %copy-start = (bf16[512,1536]{1,0:T(8,128)(2,1)}, bf16[512,1536]{1,0:T(8,128)(2,1)S(1)}, u32[]{:S(2)}) copy-start(bf16[512,1536]{1,0:T(8,128)(2,1)S(1)} %get-tuple-element.19.w_qkv) | copy-start | bytes 4718596
  5.9 0.7 copy-start.12
  6.6 40.4 %all-to-all-start = ((bf16[64,16,128]{2,1,0:T(8,128)(2,1)}), bf16[64,16,128]{2,1,0:T(8,128)(2,1)S(1)}, u32[]{:S(2)}, u32[]{:S(2)}) async-start(bf16[64,16,128]{2,1,0:T(8,128)(2,1)} %bitcast.7), calls=%async_computation | async-start | bytes 524288 | tf_op jit(solution)/shard_map/all_to_all | solution.py:331
  25.4 33.6 %collective-permute-start.2 = (s32[1,256]{1,0:T(1,128)}, s32[1,256]{1,0:T(1,128)}, u32[]{:S(2)}, u32[]{:S(2)}) collective-permute-start(s32[1,256]{1,0:T(1,128)} %bitcast.seg), channel_id=1, source_target_pairs={{0,1},{1,2},{2,3},{3,4},{4,5},{5,6},{6,7},{7,8},{8,9},{9,10},{10,1... | collective-permute-start | bytes 3080 | tf_op jit(solution)/shard_map/ppermute | solution.py:328
  29.4 29.6 %collective-permute-start.3 = (s32[1,256]{1,0:T(1,128)}, s32[1,256]{1,0:T(1,128)}, u32[]{:S(2)}, u32[]{:S(2)}) collective-permute-start(s32[1,256]{1,0:T(1,128)} %bitcast.seg), channel_id=1, source_target_pairs={{1,0},{2,1},{3,2},{4,3},{5,4},{6,5},{7,6},{8,7},{9,8},{10,9},{11,1... | collective-permute-start | bytes 3080 | tf_op jit(solution)/shard_map/ppermute | solution.py:328
  30.7 28.3 %collective-permute-start = (bf16[256,512]{1,0:T(8,128)(2,1)S(1)}, bf16[256,512]{1,0:T(8,128)(2,1)S(1)}, u32[]{:S(2)}, u32[]{:S(2)}) collective-permute-start(bf16[256,512]{1,0:T(8,128)(2,1)S(1)} %copy-done.2), channel_id=1, source_target_pairs={{0,1},{1,2},{2,3},{3,4},{4,5},{5,6},{6,7},{7,8},{8,9},{9,10},{10,1... | collective-permute-start | bytes 786440 | tf_op jit(solution)/shard_map/ppermute | solution.py:328
  35.2 23.8 %collective-permute-start.1 = (bf16[256,512]{1,0:T(8,128)(2,1)S(1)}, bf16[256,512]{1,0:T(8,128)(2,1)}, u32[]{:S(2)}, u32[]{:S(2)}) collective-permute-start(bf16[256,512]{1,0:T(8,128)(2,1)S(1)} %copy-done.2), channel_id=1, source_target_pairs={{1,0},{2,1},{3,2},{4,3},{5,4},{6,5},{7,6},{8,7},{9,8},{10,9},{11,1... | collective-permute-start | bytes 786440 | tf_op jit(solution)/shard_map/ppermute | solution.py:328
  36.6 13.3 %copy-start.10 = (s32[2]{0:T(128)}, s32[2]{0:T(128)S(1)}, u32[]{:S(2)}) copy-start(s32[2]{0:T(128)S(1)} %pad_add_fusion.where) | copy-start | bytes 28
  36.6 22.4 %copy-start.7 = (f32[2,8]{1,0:T(2,128)S(1)}, f32[2,8]{1,0:T(2,128)}, u32[]{:S(2)}) copy-start(f32[2,8]{1,0:T(2,128)} %bias.3) | copy-start | bytes 196
  47.0 1.0 copy-start.13
  50.0 24.2 %all-to-all-start.1 = ((bf16[64,8,128]{2,1,0:T(8,128)(2,1)}), bf16[64,8,128]{2,1,0:T(8,128)(2,1)S(1)}, u32[]{:S(2)}, u32[]{:S(2)}) async-start(bf16[64,8,128]{2,1,0:T(8,128)(2,1)} %combine.2), calls=%async_computation.1 | async-start | bytes 262144 | tf_op jit(solution)/shard_map/all_to_all | solution.py:331
  59.0 1.4 %copy-start.1 = (bf16[512,1536]{1,0:T(8,128)(2,1)S(1)}, bf16[512,1536]{1,0:T(8,128)(2,1)}, u32[]{:S(2)}) copy-start(bf16[512,1536]{1,0:T(8,128)(2,1)} %copy-done) | copy-start | bytes 4718596
  60.4 1.0 copy-start.14
  70.8 0.7 copy-start.3
  71.5 0.8 copy-start.18
  72.3 0.8 copy-start.21
  74.2 0.9 copy-start.6
  75.1 0.7 copy-start.9
  75.8 1.0 copy-start.19
  76.8 17.7 %copy-start.4 = (bf16[256,512]{1,0:T(8,128)(2,1)S(1)}, bf16[256,512]{1,0:T(8,128)(2,1)}, u32[]{:S(2)}) copy-start(bf16[256,512]{1,0:T(8,128)(2,1)} %copy-done.3) | copy-start | bytes 786436
  76.8 37.5 %copy-start.11 = (s32[2]{0:T(128)S(1)}, s32[2]{0:T(128)}, u32[]{:S(2)}) copy-start(s32[2]{0:T(128)} %copy-done.10) | copy-start | bytes 28
  79.7 0.7 copy-start.15
  80.5 33.8 %all-to-all-start.2 = ((bf16[64,16,128]{2,1,0:T(8,128)(2,1)}), bf16[64,16,128]{2,1,0:T(8,128)(2,1)S(1)}, u32[]{:S(2)}, u32[]{:S(2)}) async-start(bf16[64,16,128]{2,1,0:T(8,128)(2,1)} %bitcast.10), calls=%async_computation.2 | async-start | bytes 524288 | tf_op jit(solution)/shard_map/all_to_all | solution.py:331
  94.5 29.5 %collective-permute-start.4 = (bf16[256,512]{1,0:T(8,128)(2,1)S(1)}, bf16[256,512]{1,0:T(8,128)(2,1)S(1)}, u32[]{:S(2)}, u32[]{:S(2)}) collective-permute-start(bf16[256,512]{1,0:T(8,128)(2,1)S(1)} %copy-done.4), channel_id=1, source_target_pairs={{0,1},{1,2},{2,3},{3,4},{4,5},{5,6},{6,7},{7,8},{8,9},{9,10},{10,1... | collective-permute-start | bytes 786440 | tf_op jit(solution)/shard_map/ppermute | solution.py:328
  98.0 26.0 %collective-permute-start.5 = (bf16[256,512]{1,0:T(8,128)(2,1)S(1)}, bf16[256,512]{1,0:T(8,128)(2,1)S(1)}, u32[]{:S(2)}, u32[]{:S(2)}) collective-permute-start(bf16[256,512]{1,0:T(8,128)(2,1)S(1)} %copy-done.4), channel_id=1, source_target_pairs={{1,0},{2,1},{3,2},{4,3},{5,4},{6,5},{7,6},{8,7},{9,8},{10,9},{11,1... | collective-permute-start | bytes 786440 | tf_op jit(solution)/shard_map/ppermute | solution.py:328
  114.3 1.0 copy-start.16
  117.2 21.7 %all-to-all-start.3 = ((bf16[64,8,128]{2,1,0:T(8,128)(2,1)}), bf16[64,8,128]{2,1,0:T(8,128)(2,1)S(1)}, u32[]{:S(2)}, u32[]{:S(2)}) async-start(bf16[64,8,128]{2,1,0:T(8,128)(2,1)} %combine.3), calls=%async_computation.3 | async-start | bytes 262144 | tf_op jit(solution)/shard_map/all_to_all | solution.py:331
  124.0 1.0 copy-start.17
  125.0 1.0 copy-start.20
  126.0 1.0 copy-start.22
